TPU v7x, 32 devices: a whole 2x2x4 slice. The times are simulated.
32 devices in a mesh: slab: 8 (over z, y), mem: 4 (over x, core).
Axes of the slice: x: 2, y: 2, z: 4, core: 2. Of those that a mesh axis runs over, the one named last changes fastest.
Arguments:
- starting_states_set: float32 [128, 64, 1024], P('mem', 'slab'), may hold values from -6 to 6
- land_mask: int32 [64, 1024], P('slab'), may hold values 0 or 1
- cell_class: int32 [64, 1024], P('slab'), may hold values from 0 to 7
- kappa_table: float32 [8], replicated, may hold values from 0.08 to 0.2
- flow_table: float32 [2, 8], replicated, may hold values from -0.3 to 0.3
- obs_index: int32 [1024], P('slab'), may hold values from 0 to 8191
- obs_values: float32 [1024], P('slab'), may hold values from -24 to 24
- obs_var: float32 [1024], P('slab'), may hold values from 0.1 to 1
Outputs:
- analysis: float32 [128, 64, 1024], P('mem', 'slab')
All inputs are finite; a program needn't handle non-finite values. No bound on the sum of `land_mask` on one device may be relied on, other than what follows from the above.
Results may differ from a plain program's by a relative error of at most 0.00016.
Values sent between devices are 32-bit elements; how exact they have to be, the bound alone decides.
A program may use at most 64 MiB of HBM per device.

v0:
```python
import jax
import jax.numpy as jnp
from jax import lax
from jax.sharding import PartitionSpec as P

STEPS = 8
ROOT_ITERATIONS = 8
NCLS = 8


def extended(block, sides, width):
    for axis, dim in sides:
        count = lax.axis_size(axis)
        forward = [(i, i + 1) for i in range(count - 1)]
        backward = [(target, source) for source, target in forward]
        low = lax.ppermute(
            lax.slice_in_dim(block, block.shape[dim] - width, None, axis=dim), axis, forward
        )
        high = lax.ppermute(lax.slice_in_dim(block, 0, width, axis=dim), axis, backward)
        block = jnp.concatenate([low, block, high], axis=dim)
    return block


def advance(center, north, south, diffusion, flow_east, flow_north, wet_cells):
    edge = jnp.zeros_like(center[..., :1])
    east = jnp.concatenate([center[..., 1:], edge], axis=-1)
    west = jnp.concatenate([edge, center[..., :-1]], axis=-1)
    spread = north + south + east + west - 4.0 * center
    return wet_cells * (
        center
        + diffusion * spread
        - 0.5 * flow_east * (east - west)
        - 0.5 * flow_north * (north - south)
    )


def coefficients(classes, mask_rows, kappa_table, flow_table):
    diffusion = jnp.zeros(classes.shape, jnp.float32)
    flow_east = jnp.zeros(classes.shape, jnp.float32)
    flow_north = jnp.zeros(classes.shape, jnp.float32)
    for label in range(NCLS):
        hit = classes == label
        diffusion = diffusion + jnp.where(hit, kappa_table[label], 0.0)
        flow_east = flow_east + jnp.where(hit, flow_table[0, label], 0.0)
        flow_north = flow_north + jnp.where(hit, flow_table[1, label], 0.0)
    return (diffusion, flow_east, flow_north, mask_rows.astype(jnp.float32))


def statistics(observed, values, variances, factor, ens_total):
    highest = lax.Precision.HIGHEST
    ybar = jnp.sum(observed, axis=0) / ens_total
    err = variances * factor
    anom = (observed - ybar) / jnp.sqrt(err * (ens_total - 1.0))
    dev = (values - ybar) / jnp.sqrt(err)
    return (jnp.dot(anom, anom.T, precision=highest), jnp.dot(anom, dev, precision=highest))


def local(
    starting_states_set,
    land_mask,
    cell_class,
    kappa_table,
    flow_table,
    obs_index,
    obs_values,
    obs_var,
):
    highest = lax.Precision.HIGHEST
    kd = starting_states_set.shape[0]
    rows = starting_states_set.shape[1]
    ens_total = kd * lax.axis_size("mem")
    current_profile = starting_states_set
    diffusion, flow_east, flow_north, wet_cells = coefficients(
        cell_class, land_mask, kappa_table, flow_table
    )
    for step in range(STEPS):
        padded = extended(current_profile, (("slab", 1),), 1)
        current_profile = advance(
            padded[:, 1:-1],
            padded[:, 2:],
            padded[:, :-2],
            diffusion,
            flow_east,
            flow_north,
            wet_cells,
        )
    raveled_vector = current_profile.reshape(kd, rows * current_profile.shape[2])
    observed = jnp.take(raveled_vector, obs_index, axis=1)
    slab_here = lax.axis_index("slab").astype(jnp.float32)
    factor = 1.0 + 2.0 * slab_here / float(lax.axis_size("slab") - 1)
    member_group = lax.axis_index("mem")
    columns = lax.all_to_all(observed, "mem", split_axis=1, concat_axis=0, tiled=True)
    count = columns.shape[1]
    values = lax.dynamic_slice_in_dim(obs_values, member_group * count, count)
    variances = lax.dynamic_slice_in_dim(obs_var, member_group * count, count)
    gram_part, proj_part = statistics(columns, values, variances, factor, ens_total)
    gram, proj = lax.psum((gram_part, proj_part), ("slab", "mem"))
    ident = jnp.eye(ens_total, dtype=jnp.float32)
    matrix = ident + gram
    scale = jnp.trace(matrix)
    upper = matrix / scale
    lower = ident
    for turn in range(ROOT_ITERATIONS):
        factor_q = 1.5 * ident - 0.5 * jnp.dot(lower, upper, precision=highest)
        upper = jnp.dot(upper, factor_q, precision=highest)
        lower = jnp.dot(factor_q, lower, precision=highest)
    transform_weights = lower / jnp.sqrt(scale)
    mean_w = jnp.dot(lower, jnp.dot(lower, proj, precision=highest), precision=highest) / (
        scale * jnp.sqrt(ens_total - 1.0)
    )
    total_w = transform_weights + mean_w[:, None]
    omega = 1.0 / ens_total + total_w - (jnp.sum(total_w, axis=0) / ens_total)[None, :]
    mixed = jnp.einsum(
        "ij,irc->jrc",
        omega,
        lax.all_to_all(current_profile, "mem", split_axis=2, concat_axis=0, tiled=True),
        precision=highest,
    )
    return lax.all_to_all(mixed, "mem", split_axis=0, concat_axis=2, tiled=True)


def solution(mesh):
    return jax.shard_map(
        local,
        mesh=mesh,
        in_specs=(
            P("mem", "slab", None),
            P("slab", None),
            P("slab", None),
            P(),
            P(),
            P("slab"),
            P("slab"),
            P("slab"),
        ),
        out_specs=P("mem", "slab", None),
        check_vma=False,
    )
```

profile of v0, /device:TPU:0, one launch (start us, length us, event | category | flops | bytes accessed | tf_op | source)
XLA Modules:
  0.0 308.6 jit_solution(16976725727790895447)
XLA Ops:
  6.5 1.9 copy.42
  8.4 0.7 fusion.44
  9.2 1.3 collective-permute-start
  10.5 5.5 %collective-permute-start.1 = (f32[32,1,1024]{2,0,1:T(8,128)}, f32[32,1,1024]{2,0,1:T(8,128)S(1)}, u32[]{:S(2)}, u32[]{:S(2)}) collective-permute-start(f32[32,1,1024]{2,0,1:T(8,128)} %get-tuple-element.42), channel_id=1, source_target_pairs={{0,4},{4,8},{8,12},{12,16},{16,20},{20,24},{24,28},{1,5},{5,9},{9,... | collective-permute-start | bytes 393224 | tf_op jit(solution)/shard_map/ppermute | solution.py:16
  16.4 0.7 fusion.47
  17.0 0.7 fusion.46
  17.8 5.0 %select_add_fusion = (f32[8,1024]{1,0:T(8,128)S(1)}, pred[8,1024]{1,0:T(8,128)(4,1)S(1)}, pred[8,1024]{1,0:T(8,128)(4,1)S(1)}, pred[8,1024]{1,0:T(8,128)(4,1)S(1...) fusion(f32[]{:T(128)} %bitcast.7, f32[]{:T(128)} %bitcast.6, ...), kind=kLoop, calls=%fused_computation.61 | loop fusion | flops 188416 | bytes 131104 | tf_op jit(solution)/shard_map/add | solution.py:43
  22.8 5.0 %add_multiply_fusion = f32[8,1024]{1,0:T(8,128)S(1)} fusion(pred[8,1024]{1,0:T(8,128)(4,1)S(1)} %get-tuple-element.13, pred[8,1024]{1,0:T(8,128)(4,1)S(1)} %get-tuple-element.12, pred[8,1024]{1,0:T(8,128)(4,1)S(1)} %get-tuple-element.11, pred[8,1024]{1,0:T(8,128)(4,1)S(1)} %get-tuple-element.10, pred[8,1024]{1,0:T(8,128)(4,1)S(1)} %get-tuple-element.9, ...), kind=kLoop, calls=%fused_computation.59 | loop fusion | flops 131072 | bytes 98336 | tf_op jit(solution)/shard_map/mul | solution.py:33
  27.8 5.0 %add_multiply_fusion.1 = f32[8,1024]{1,0:T(8,128)S(1)} fusion(pred[8,1024]{1,0:T(8,128)(4,1)S(1)} %get-tuple-element.13, pred[8,1024]{1,0:T(8,128)(4,1)S(1)} %get-tuple-element.12, pred[8,1024]{1,0:T(8,128)(4,1)S(1)} %get-tuple-element.11, pred[8,1024]{1,0:T(8,128)(4,1)S(1)} %get-tuple-element.10, pred[8,1024]{1,0:T(8,128)(4,1)S(1)} %get-tuple-element.9, ...), kind=kLoop, calls=%fused_computation.60 | loop fusion | flops 131072 | bytes 98336 | tf_op jit(solution)/shard_map/mul | solution.py:32
  33.0 0.6 subtract_multiply_fusion.7
  33.7 1.3 collective-permute-start.2
  35.0 5.4 %collective-permute-start.3 = (f32[32,1,1024]{2,0,1:T(8,128)S(1)}, f32[32,1,1024]{2,0,1:T(8,128)S(1)}, u32[]{:S(2)}, u32[]{:S(2)}) collective-permute-start(f32[32,1,1024]{2,0,1:T(8,128)S(1)} %get-tuple-element.38), channel_id=1, source_target_pairs={{0,4},{4,8},{8,12},{12,16},{16,20},{20,24},{24,28},{1,5},{5,9},{9,... | collective-permute-start | bytes 393224 | tf_op jit(solution)/shard_map/ppermute | solution.py:16
  41.4 2.9 collective-permute-done.3
  44.4 0.7 subtract_multiply_fusion.6
  45.1 1.3 collective-permute-start.4
  46.4 5.0 %collective-permute-start.5 = (f32[32,1,1024]{2,0,1:T(8,128)S(1)}, f32[32,1,1024]{2,0,1:T(8,128)S(1)}, u32[]{:S(2)}, u32[]{:S(2)}) collective-permute-start(f32[32,1,1024]{2,0,1:T(8,128)S(1)} %get-tuple-element.34), channel_id=1, source_target_pairs={{0,4},{4,8},{8,12},{12,16},{16,20},{20,24},{24,28},{1,5},{5,9},{9,... | collective-permute-start | bytes 393224 | tf_op jit(solution)/shard_map/ppermute | solution.py:16
  51.8 1.1 collective-permute-done.4
  52.9 3.0 collective-permute-done.5
  55.8 0.7 subtract_multiply_fusion.5
  56.5 1.3 collective-permute-start.6
  57.8 5.0 %collective-permute-start.7 = (f32[32,1,1024]{2,0,1:T(8,128)S(1)}, f32[32,1,1024]{2,0,1:T(8,128)S(1)}, u32[]{:S(2)}, u32[]{:S(2)}) collective-permute-start(f32[32,1,1024]{2,0,1:T(8,128)S(1)} %get-tuple-element.30), channel_id=1, source_target_pairs={{0,4},{4,8},{8,12},{12,16},{16,20},{20,24},{24,28},{1,5},{5,9},{9,... | collective-permute-start | bytes 393224 | tf_op jit(solution)/shard_map/ppermute | solution.py:16
  63.3 1.3 collective-permute-done.6
  64.6 3.0 collective-permute-done.7
  67.5 0.7 subtract_multiply_fusion.4
  68.2 1.3 collective-permute-start.8
  69.5 5.0 %collective-permute-start.9 = (f32[32,1,1024]{2,0,1:T(8,128)S(1)}, f32[32,1,1024]{2,0,1:T(8,128)S(1)}, u32[]{:S(2)}, u32[]{:S(2)}) collective-permute-start(f32[32,1,1024]{2,0,1:T(8,128)S(1)} %get-tuple-element.26), channel_id=1, source_target_pairs={{0,4},{4,8},{8,12},{12,16},{16,20},{20,24},{24,28},{1,5},{5,9},{9,... | collective-permute-start | bytes 393224 | tf_op jit(solution)/shard_map/ppermute | solution.py:16
  75.0 1.3 collective-permute-done.8
  76.3 3.0 collective-permute-done.9
  79.3 0.7 subtract_multiply_fusion.3
  80.0 1.3 collective-permute-start.10
  81.3 5.0 %collective-permute-start.11 = (f32[32,1,1024]{2,0,1:T(8,128)S(1)}, f32[32,1,1024]{2,0,1:T(8,128)S(1)}, u32[]{:S(2)}, u32[]{:S(2)}) collective-permute-start(f32[32,1,1024]{2,0,1:T(8,128)S(1)} %get-tuple-element.22), channel_id=1, source_target_pairs={{0,4},{4,8},{8,12},{12,16},{16,20},{20,24},{24,28},{1,5},{5,9},{9,... | collective-permute-start | bytes 393224 | tf_op jit(solution)/shard_map/ppermute | solution.py:16
  86.7 1.3 collective-permute-done.10
  88.0 3.0 collective-permute-done.11
  91.0 0.7 subtract_multiply_fusion.2
  91.7 1.3 collective-permute-start.12
  93.0 5.0 %collective-permute-start.13 = (f32[32,1,1024]{2,0,1:T(8,128)S(1)}, f32[32,1,1024]{2,0,1:T(8,128)S(1)}, u32[]{:S(2)}, u32[]{:S(2)}) collective-permute-start(f32[32,1,1024]{2,0,1:T(8,128)S(1)} %get-tuple-element.18), channel_id=1, source_target_pairs={{0,4},{4,8},{8,12},{12,16},{16,20},{20,24},{24,28},{1,5},{5,9},{9,... | collective-permute-start | bytes 393224 | tf_op jit(solution)/shard_map/ppermute | solution.py:16
  98.4 1.3 collective-permute-done.12
  99.7 3.0 collective-permute-done.13
  102.7 0.7 subtract_multiply_fusion.1
  103.4 1.3 collective-permute-start.14
  104.7 5.0 %collective-permute-start.15 = (f32[32,1,1024]{2,0,1:T(8,128)S(1)}, f32[32,1,1024]{2,0,1:T(8,128)S(1)}, u32[]{:S(2)}, u32[]{:S(2)}) collective-permute-start(f32[32,1,1024]{2,0,1:T(8,128)S(1)} %get-tuple-element.14), channel_id=1, source_target_pairs={{0,4},{4,8},{8,12},{12,16},{16,20},{20,24},{24,28},{1,5},{5,9},{9,... | collective-permute-start | bytes 393224 | tf_op jit(solution)/shard_map/ppermute | solution.py:16
  110.1 1.3 collective-permute-done.14
  111.5 3.0 collective-permute-done.15
  114.4 0.7 subtract_multiply_fusion
  115.1 2.6 copy.43
  117.7 2.8 gather_fusion
  120.7 0.7 reshape.69
  121.4 3.4 %all-to-all-start = ((f32[4,1,1024]{2,1,0:T(1,128)}), f32[4,1,1024]{2,1,0:T(1,128)S(1)}, u32[]{:S(2)}, u32[]{:S(2)}) async-start(f32[4,1,1024]{2,1,0:T(1,128)} %reshape.69), calls=%async_computation | async-start | bytes 32768 | tf_op jit(solution)/shard_map/all_to_all | solution.py:92
  124.9 2.7 copy.46
  127.6 4.8 %reshape.67 = f32[4,1,65536]{2,1,0:T(1,128)} reshape(f32[1024,8,32]{2,1,0:T(8,128)} %bitcast.117) | data formatting | bytes 2097152
  132.4 3.5 %all-to-all-start.1 = ((f32[4,1,65536]{2,1,0:T(1,128)}), f32[4,1,65536]{2,1,0:T(1,128)S(1)}, u32[]{:S(2)}, u32[]{:S(2)}) async-start(f32[4,1,65536]{2,1,0:T(1,128)} %reshape.67), calls=%async_computation.1 | async-start | bytes 2097152 | tf_op jit(solution)/shard_map/all_to_all | solution.py:116
  136.6 0.7 reduce.3
  137.9 0.9 fusion.49
  139.1 44.7 %psum.15 = f32[128]{0:T(128)S(1)} all-reduce(f32[128]{0:T(128)S(1)} %convolution_bitcast_fusion.2), channel_id=1, replica_groups=mesh['slab'=8,'mem'=4] {'slab','mem'}, use_global_device_ids=true, to_apply=%region_3.4 | all-reduce | flops 128 | bytes 1024 | tf_op jit(solution)/shard_map/psum | solution.py:97
  183.8 76.2 %all-reduce.18.cloned.1.call-done = f32[128,128]{1,0:T(8,128)} async-done(((f32[128,128]{1,0:T(8,128)}), f32[128,128]{1,0:T(8,128)}) %all-reduce.18.cloned.1.call-update) | async-done | bytes 65552 | tf_op jit(solution)/shard_map/psum | solution.py:97
  259.9 1.5 select_reduce_fusion
  261.4 1.6 fusion.7
  263.2 1.6 fusion.17
  270.8 3.7 %reduce.2 = f32[4,65536]{1,0:T(4,128)S(1)} reduce(f32[4,1,65536]{2,1,0:T(1,128)S(1)} %all-to-all-done.1, f32[]{:T(128)} %broadcast.130), dimensions={1}, to_apply=%all_to_all.41.reduce_sub_computation | reduce | bytes 2097156 | tf_op jit(solution)/shard_map/all_to_all | solution.py:116
  274.5 3.4 %reshape.68 = f32[1024,8,32]{2,1,0:T(8,128)} reshape(f32[4,65536]{1,0:T(4,128)S(1)} %reduce.2) | data formatting | bytes 2097152
  277.9 2.8 copy.47
  280.7 1.1 fusion.9
  282.4 18.2 %all_to_all.52 = f32[128,8,256]{2,1,0:T(8,128)S(1)} all-to-all(f32[128,8,256]{2,1,0:T(8,128)S(1)} %copy.49), channel_id=1, replica_groups=mesh['slab'=8,'mem'=4] {'mem'}, dimensions={0} | all-to-all | bytes 2097152 | tf_op jit(solution)/shard_map/all_to_all | solution.py:119
  300.6 1.1 copy.50
  (80 shorter events, 11.0 us)
Async XLA Ops:
  6.5 9.8 %copy-start.2 = (f32[8]{0:T(128)S(1)}, f32[8]{0:T(128)}, u32[]{:S(2)}) copy-start(f32[8]{0:T(128)} %param.11) | copy-start | bytes 100
  6.5 10.5 %copy-start = (f32[2,8]{1,0:T(2,128)S(1)}, f32[2,8]{1,0:T(2,128)}, u32[]{:S(2)}) copy-start(f32[2,8]{1,0:T(2,128)} %param.12) | copy-start | bytes 196
  6.5 11.2 %copy-start.5 = (s32[128]{0:T(128)S(1)}, s32[128]{0:T(128)}, u32[]{:S(2)}) copy-start(s32[128]{0:T(128)} %param.13) | copy-start | bytes 1540
  6.5 11.2 %copy-start.3 = (s32[8,1024]{1,0:T(8,128)S(1)}, s32[8,1024]{1,0:T(8,128)}, u32[]{:S(2)}) copy-start(s32[8,1024]{1,0:T(8,128)} %param.10) | copy-start | bytes 98308
  6.5 26.3 %copy-start.1 = (s32[8,1024]{1,0:T(8,128)S(1)}, s32[8,1024]{1,0:T(8,128)}, u32[]{:S(2)}) copy-start(s32[8,1024]{1,0:T(8,128)} %param.9) | copy-start | bytes 98308
  9.2 23.8 %collective-permute-start = (f32[32,1,1024]{2,0,1:T(8,128)}, f32[32,1,1024]{2,0,1:T(8,128)S(1)}, u32[]{:S(2)}, u32[]{:S(2)}) collective-permute-start(f32[32,1,1024]{2,0,1:T(8,128)} %get-tuple-element.43), channel_id=1, source_target_pairs={{4,0},{8,4},{12,8},{16,12},{20,16},{24,20},{28,24},{5,1},{9,5},{13... | collective-permute-start | bytes 393224 | tf_op jit(solution)/shard_map/ppermute | solution.py:19
  10.5 22.5 %collective-permute-start.1 = (f32[32,1,1024]{2,0,1:T(8,128)}, f32[32,1,1024]{2,0,1:T(8,128)S(1)}, u32[]{:S(2)}, u32[]{:S(2)}) collective-permute-start(f32[32,1,1024]{2,0,1:T(8,128)} %get-tuple-element.42), channel_id=1, source_target_pairs={{0,4},{4,8},{8,12},{12,16},{16,20},{20,24},{24,28},{1,5},{5,9},{9,... | collective-permute-start | bytes 393224 | tf_op jit(solution)/shard_map/ppermute | solution.py:16
  33.7 7.8 %collective-permute-start.2 = (f32[32,1,1024]{2,0,1:T(8,128)S(1)}, f32[32,1,1024]{2,0,1:T(8,128)S(1)}, u32[]{:S(2)}, u32[]{:S(2)}) collective-permute-start(f32[32,1,1024]{2,0,1:T(8,128)S(1)} %get-tuple-element.39), channel_id=1, source_target_pairs={{4,0},{8,4},{12,8},{16,12},{20,16},{24,20},{28,24},{5,1},{9,5},{13... | collective-permute-start | bytes 393224 | tf_op jit(solution)/shard_map/ppermute | solution.py:19
  35.0 9.4 %collective-permute-start.3 = (f32[32,1,1024]{2,0,1:T(8,128)S(1)}, f32[32,1,1024]{2,0,1:T(8,128)S(1)}, u32[]{:S(2)}, u32[]{:S(2)}) collective-permute-start(f32[32,1,1024]{2,0,1:T(8,128)S(1)} %get-tuple-element.38), channel_id=1, source_target_pairs={{0,4},{4,8},{8,12},{12,16},{16,20},{20,24},{24,28},{1,5},{5,9},{9,... | collective-permute-start | bytes 393224 | tf_op jit(solution)/shard_map/ppermute | solution.py:16
  45.1 7.8 %collective-permute-start.4 = (f32[32,1,1024]{2,0,1:T(8,128)S(1)}, f32[32,1,1024]{2,0,1:T(8,128)S(1)}, u32[]{:S(2)}, u32[]{:S(2)}) collective-permute-start(f32[32,1,1024]{2,0,1:T(8,128)S(1)} %get-tuple-element.35), channel_id=1, source_target_pairs={{4,0},{8,4},{12,8},{16,12},{20,16},{24,20},{28,24},{5,1},{9,5},{13... | collective-permute-start | bytes 393224 | tf_op jit(solution)/shard_map/ppermute | solution.py:19
  46.4 9.5 %collective-permute-start.5 = (f32[32,1,1024]{2,0,1:T(8,128)S(1)}, f32[32,1,1024]{2,0,1:T(8,128)S(1)}, u32[]{:S(2)}, u32[]{:S(2)}) collective-permute-start(f32[32,1,1024]{2,0,1:T(8,128)S(1)} %get-tuple-element.34), channel_id=1, source_target_pairs={{0,4},{4,8},{8,12},{12,16},{16,20},{20,24},{24,28},{1,5},{5,9},{9,... | collective-permute-start | bytes 393224 | tf_op jit(solution)/shard_map/ppermute | solution.py:16
  56.5 8.1 %collective-permute-start.6 = (f32[32,1,1024]{2,0,1:T(8,128)S(1)}, f32[32,1,1024]{2,0,1:T(8,128)S(1)}, u32[]{:S(2)}, u32[]{:S(2)}) collective-permute-start(f32[32,1,1024]{2,0,1:T(8,128)S(1)} %get-tuple-element.31), channel_id=1, source_target_pairs={{4,0},{8,4},{12,8},{16,12},{20,16},{24,20},{28,24},{5,1},{9,5},{13... | collective-permute-start | bytes 393224 | tf_op jit(solution)/shard_map/ppermute | solution.py:19
  57.8 9.7 %collective-permute-start.7 = (f32[32,1,1024]{2,0,1:T(8,128)S(1)}, f32[32,1,1024]{2,0,1:T(8,128)S(1)}, u32[]{:S(2)}, u32[]{:S(2)}) collective-permute-start(f32[32,1,1024]{2,0,1:T(8,128)S(1)} %get-tuple-element.30), channel_id=1, source_target_pairs={{0,4},{4,8},{8,12},{12,16},{16,20},{20,24},{24,28},{1,5},{5,9},{9,... | collective-permute-start | bytes 393224 | tf_op jit(solution)/shard_map/ppermute | solution.py:16
  68.2 8.1 %collective-permute-start.8 = (f32[32,1,1024]{2,0,1:T(8,128)S(1)}, f32[32,1,1024]{2,0,1:T(8,128)S(1)}, u32[]{:S(2)}, u32[]{:S(2)}) collective-permute-start(f32[32,1,1024]{2,0,1:T(8,128)S(1)} %get-tuple-element.27), channel_id=1, source_target_pairs={{4,0},{8,4},{12,8},{16,12},{20,16},{24,20},{28,24},{5,1},{9,5},{13... | collective-permute-start | bytes 393224 | tf_op jit(solution)/shard_map/ppermute | solution.py:19
  69.5 9.7 %collective-permute-start.9 = (f32[32,1,1024]{2,0,1:T(8,128)S(1)}, f32[32,1,1024]{2,0,1:T(8,128)S(1)}, u32[]{:S(2)}, u32[]{:S(2)}) collective-permute-start(f32[32,1,1024]{2,0,1:T(8,128)S(1)} %get-tuple-element.26), channel_id=1, source_target_pairs={{0,4},{4,8},{8,12},{12,16},{16,20},{20,24},{24,28},{1,5},{5,9},{9,... | collective-permute-start | bytes 393224 | tf_op jit(solution)/shard_map/ppermute | solution.py:16
  80.0 8.1 %collective-permute-start.10 = (f32[32,1,1024]{2,0,1:T(8,128)S(1)}, f32[32,1,1024]{2,0,1:T(8,128)S(1)}, u32[]{:S(2)}, u32[]{:S(2)}) collective-permute-start(f32[32,1,1024]{2,0,1:T(8,128)S(1)} %get-tuple-element.23), channel_id=1, source_target_pairs={{4,0},{8,4},{12,8},{16,12},{20,16},{24,20},{28,24},{5,1},{9,5},{13... | collective-permute-start | bytes 393224 | tf_op jit(solution)/shard_map/ppermute | solution.py:19
  81.3 9.7 %collective-permute-start.11 = (f32[32,1,1024]{2,0,1:T(8,128)S(1)}, f32[32,1,1024]{2,0,1:T(8,128)S(1)}, u32[]{:S(2)}, u32[]{:S(2)}) collective-permute-start(f32[32,1,1024]{2,0,1:T(8,128)S(1)} %get-tuple-element.22), channel_id=1, source_target_pairs={{0,4},{4,8},{8,12},{12,16},{16,20},{20,24},{24,28},{1,5},{5,9},{9,... | collective-permute-start | bytes 393224 | tf_op jit(solution)/shard_map/ppermute | solution.py:16
  91.7 8.1 %collective-permute-start.12 = (f32[32,1,1024]{2,0,1:T(8,128)S(1)}, f32[32,1,1024]{2,0,1:T(8,128)S(1)}, u32[]{:S(2)}, u32[]{:S(2)}) collective-permute-start(f32[32,1,1024]{2,0,1:T(8,128)S(1)} %get-tuple-element.19), channel_id=1, source_target_pairs={{4,0},{8,4},{12,8},{16,12},{20,16},{24,20},{28,24},{5,1},{9,5},{13... | collective-permute-start | bytes 393224 | tf_op jit(solution)/shard_map/ppermute | solution.py:19
  93.0 9.7 %collective-permute-start.13 = (f32[32,1,1024]{2,0,1:T(8,128)S(1)}, f32[32,1,1024]{2,0,1:T(8,128)S(1)}, u32[]{:S(2)}, u32[]{:S(2)}) collective-permute-start(f32[32,1,1024]{2,0,1:T(8,128)S(1)} %get-tuple-element.18), channel_id=1, source_target_pairs={{0,4},{4,8},{8,12},{12,16},{16,20},{20,24},{24,28},{1,5},{5,9},{9,... | collective-permute-start | bytes 393224 | tf_op jit(solution)/shard_map/ppermute | solution.py:16
  103.4 8.1 %collective-permute-start.14 = (f32[32,1,1024]{2,0,1:T(8,128)S(1)}, f32[32,1,1024]{2,0,1:T(8,128)S(1)}, u32[]{:S(2)}, u32[]{:S(2)}) collective-permute-start(f32[32,1,1024]{2,0,1:T(8,128)S(1)} %get-tuple-element.15), channel_id=1, source_target_pairs={{4,0},{8,4},{12,8},{16,12},{20,16},{24,20},{28,24},{5,1},{9,5},{13... | collective-permute-start | bytes 393224 | tf_op jit(solution)/shard_map/ppermute | solution.py:19
  104.7 9.7 %collective-permute-start.15 = (f32[32,1,1024]{2,0,1:T(8,128)S(1)}, f32[32,1,1024]{2,0,1:T(8,128)S(1)}, u32[]{:S(2)}, u32[]{:S(2)}) collective-permute-start(f32[32,1,1024]{2,0,1:T(8,128)S(1)} %get-tuple-element.14), channel_id=1, source_target_pairs={{0,4},{4,8},{8,12},{12,16},{16,20},{20,24},{24,28},{1,5},{5,9},{9,... | collective-permute-start | bytes 393224 | tf_op jit(solution)/shard_map/ppermute | solution.py:16
  114.4 10.4 %copy-start.4 = (f32[128]{0:T(128)S(1)}, f32[128]{0:T(128)}, u32[]{:S(2)}) copy-start(f32[128]{0:T(128)} %param.15) | copy-start | bytes 1540
  121.4 11.1 %all-to-all-start = ((f32[4,1,1024]{2,1,0:T(1,128)}), f32[4,1,1024]{2,1,0:T(1,128)S(1)}, u32[]{:S(2)}, u32[]{:S(2)}) async-start(f32[4,1,1024]{2,1,0:T(1,128)} %reshape.69), calls=%async_computation | async-start | bytes 32768 | tf_op jit(solution)/shard_map/all_to_all | solution.py:92
  127.6 11.3 %copy-start.6 = (f32[128]{0:T(128)S(1)}, f32[128]{0:T(128)}, u32[]{:S(2)}) copy-start(f32[128]{0:T(128)} %param.14) | copy-start | bytes 1540
  132.4 138.3 %all-to-all-start.1 = ((f32[4,1,65536]{2,1,0:T(1,128)}), f32[4,1,65536]{2,1,0:T(1,128)S(1)}, u32[]{:S(2)}, u32[]{:S(2)}) async-start(f32[4,1,65536]{2,1,0:T(1,128)} %reshape.67), calls=%async_computation.1 | async-start | bytes 2097152 | tf_op jit(solution)/shard_map/all_to_all | solution.py:116
  136.0 124.0 %all-reduce.18.cloned.1.call-start = ((), (), s32[]{:S(2)}) async-start(), calls=%async_computation.3 | async-start | bytes 131072 | tf_op jit(solution)/shard_map/psum | solution.py:97
Sparse Core Ops, SparseCore 0:
  142.4 117.4 all-reduce.17
where the time goes:
time: 310 us; the launch traced here: 309 us
  waiting for transfers between devices  105 us (34%)
  blocking collectives  62.9 us (20%)
  starting transfers between devices  58.4 us (19%)
  local copies, waits for them, and re-layouts  29.9 us (10%)
  other arithmetic  26.7 us (9%)
  between operations  15.3 us (5%)
  matrix products  10.1 us (3%)
    psum x1, waiting for transfers between devices, local(): gram, proj = lax.psum((gram_part, proj_part), ('slab', 'mem'))  76.2 us
    psum x1, blocking collectives, local(): gram, proj = lax.psum((gram_part, proj_part), ('slab', 'mem'))  44.7 us
    ppermute x8, starting transfers between devices, extended(): lax.ppermute(lax.slice_in_dim(block, block.shape[dim] - width, None, axis...  41.1 us
    ppermute x8, waiting for transfers between devices, extended(): lax.ppermute(lax.slice_in_dim(block, block.shape[dim] - width, None, axis...  20.7 us
    all_to_all x1, blocking collectives, local(): return lax.all_to_all(mixed, 'mem', split_axis=0, concat_axis=2, tiled=True)  18.2 us
    unnamed x19, local copies, waits for them, and re-layouts  10.9 us
    ppermute x8, starting transfers between devices, extended(): lax.ppermute(lax.slice_in_dim(block, 0, width, axis=dim), axis, backward)  10.3 us
    ppermute x8, waiting for transfers between devices, extended(): lax.ppermute(lax.slice_in_dim(block, 0, width, axis=dim), axis, backward)  8.4 us
  transfers between devices with their start and end apart: 19, of which 15 were waited for; matrix products, arithmetic and copies ran while one was open for 13% of the time, Pallas kernels for 0%

commit v1 on v0

--- a/solution.py
+++ b/solution.py
@@ -113,7 +113,12 @@
     mixed = jnp.einsum(
         "ij,irc->jrc",
         omega,
-        lax.all_to_all(current_profile, "mem", split_axis=2, concat_axis=0, tiled=True),
+        jnp.concatenate(
+            lax.all_to_all(
+                jnp.stack(jnp.split(current_profile, lax.axis_size("mem"), axis=2)), "mem", 0, 0
+            ),
+            axis=0,
+        ),
         precision=highest,
     )
     return lax.all_to_all(mixed, "mem", split_axis=0, concat_axis=2, tiled=True)

time: 310 us -> 299 us (0.965)
  local copies, waits for them, and re-layouts: 29.9 us -> 17 us
    unnamed x19 -> x17, local copies, waits for them, and re-layouts: 10.9 us -> 2.71 us
    all_to_all x1 -> x0, other arithmetic: 3.71 us -> none  [local(): lax.all_to_all(current_profile, 'mem', split_axis=2, concat_axis=0, tiled...]
    all_to_all x2 -> x1, local copies, waits for them, and re-layouts: 3.38 us -> 0.08 us  [local(): lax.all_to_all(jnp.stack(jnp.split(current_profile, lax.axis_size('mem'),...]
  transfers between devices with their start and end apart: 19 -> 19, of which waited for: 15 -> 16; matrix products, arithmetic and copies ran while one was open for 13% -> 12% of each run, Pallas kernels for 0% -> 0%
where the time goes in v1:
time: 299 us; the launch traced here: 297 us
  waiting for transfers between devices  108 us (36%)
  blocking collectives  62.9 us (21%)
  starting transfers between devices  58.4 us (20%)
  other arithmetic  25.3 us (8%)
  local copies, waits for them, and re-layouts  17 us (6%)
  between operations  15.5 us (5%)
  matrix products  10.3 us (3%)
    psum x1, waiting for transfers between devices, local(): gram, proj = lax.psum((gram_part, proj_part), ('slab', 'mem'))  76.2 us
    psum x1, blocking collectives, local(): gram, proj = lax.psum((gram_part, proj_part), ('slab', 'mem'))  44.7 us
    ppermute x8, starting transfers between devices, extended(): lax.ppermute(lax.slice_in_dim(block, block.shape[dim] - width, None, axis...  41.1 us
    ppermute x8, waiting for transfers between devices, extended(): lax.ppermute(lax.slice_in_dim(block, block.shape[dim] - width, None, axis...  20.7 us
    all_to_all x1, blocking collectives, local(): return lax.all_to_all(mixed, 'mem', split_axis=0, concat_axis=2, tiled=True)  18.2 us
    ppermute x8, starting transfers between devices, extended(): lax.ppermute(lax.slice_in_dim(block, 0, width, axis=dim), axis, backward)  10.3 us
    ppermute x8, waiting for transfers between devices, extended(): lax.ppermute(lax.slice_in_dim(block, 0, width, axis=dim), axis, backward)  8.4 us
  transfers between devices with their start and end apart: 19, of which 16 were waited for; matrix products, arithmetic and copies ran while one was open for 12% of the time, Pallas kernels for 0%

profile of v1, /device:TPU:0, one launch (start us, length us, event | category | flops | bytes accessed | tf_op | source)
XLA Modules:
  0.0 297.3 jit_solution(5623991947786902906)
XLA Ops:
  6.6 1.9 copy.26
  8.5 0.7 fusion.44
  9.2 1.3 collective-permute-start
  10.5 5.5 %collective-permute-start.1 = (f32[32,1,1024]{2,0,1:T(8,128)}, f32[32,1,1024]{2,0,1:T(8,128)S(1)}, u32[]{:S(2)}, u32[]{:S(2)}) collective-permute-start(f32[32,1,1024]{2,0,1:T(8,128)} %get-tuple-element.46), channel_id=1, source_target_pairs={{0,4},{4,8},{8,12},{12,16},{16,20},{20,24},{24,28},{1,5},{5,9},{9,... | collective-permute-start | bytes 393224 | tf_op jit(solution)/shard_map/ppermute | solution.py:16
  17.0 0.7 fusion.47
  17.6 0.7 fusion.46
  18.3 4.9 %select_add_fusion = (f32[8,1024]{1,0:T(8,128)S(1)}, pred[8,1024]{1,0:T(8,128)(4,1)S(1)}, pred[8,1024]{1,0:T(8,128)(4,1)S(1)}, pred[8,1024]{1,0:T(8,128)(4,1)S(1...) fusion(f32[]{:T(128)} %bitcast.7, f32[]{:T(128)} %bitcast.6, ...), kind=kLoop, calls=%fused_computation.66 | loop fusion | flops 188416 | bytes 131104 | tf_op jit(solution)/shard_map/add | solution.py:43
  23.3 5.0 %add_multiply_fusion = f32[8,1024]{1,0:T(8,128)S(1)} fusion(pred[8,1024]{1,0:T(8,128)(4,1)S(1)} %get-tuple-element.13, pred[8,1024]{1,0:T(8,128)(4,1)S(1)} %get-tuple-element.12, pred[8,1024]{1,0:T(8,128)(4,1)S(1)} %get-tuple-element.11, pred[8,1024]{1,0:T(8,128)(4,1)S(1)} %get-tuple-element.10, pred[8,1024]{1,0:T(8,128)(4,1)S(1)} %get-tuple-element.9, ...), kind=kLoop, calls=%fused_computation.64 | loop fusion | flops 131072 | bytes 98336 | tf_op jit(solution)/shard_map/mul | solution.py:33
  28.3 5.1 %add_multiply_fusion.1 = f32[8,1024]{1,0:T(8,128)S(1)} fusion(pred[8,1024]{1,0:T(8,128)(4,1)S(1)} %get-tuple-element.13, pred[8,1024]{1,0:T(8,128)(4,1)S(1)} %get-tuple-element.12, pred[8,1024]{1,0:T(8,128)(4,1)S(1)} %get-tuple-element.11, pred[8,1024]{1,0:T(8,128)(4,1)S(1)} %get-tuple-element.10, pred[8,1024]{1,0:T(8,128)(4,1)S(1)} %get-tuple-element.9, ...), kind=kLoop, calls=%fused_computation.65 | loop fusion | flops 131072 | bytes 98336 | tf_op jit(solution)/shard_map/mul | solution.py:32
  33.4 0.8 convert_element_type.10
  34.2 0.7 broadcast_in_dim.152
  35.0 0.6 subtract_multiply_fusion.7
  35.6 1.3 collective-permute-start.2
  36.9 5.4 %collective-permute-start.3 = (f32[32,1,1024]{2,0,1:T(8,128)S(1)}, f32[32,1,1024]{2,0,1:T(8,128)S(1)}, u32[]{:S(2)}, u32[]{:S(2)}) collective-permute-start(f32[32,1,1024]{2,0,1:T(8,128)S(1)} %get-tuple-element.42), channel_id=1, source_target_pairs={{0,4},{4,8},{8,12},{12,16},{16,20},{20,24},{24,28},{1,5},{5,9},{9,... | collective-permute-start | bytes 393224 | tf_op jit(solution)/shard_map/ppermute | solution.py:16
  43.4 2.9 collective-permute-done.3
  46.3 0.7 subtract_multiply_fusion.6
  47.0 1.3 collective-permute-start.4
  48.3 5.0 %collective-permute-start.5 = (f32[32,1,1024]{2,0,1:T(8,128)S(1)}, f32[32,1,1024]{2,0,1:T(8,128)S(1)}, u32[]{:S(2)}, u32[]{:S(2)}) collective-permute-start(f32[32,1,1024]{2,0,1:T(8,128)S(1)} %get-tuple-element.38), channel_id=1, source_target_pairs={{0,4},{4,8},{8,12},{12,16},{16,20},{20,24},{24,28},{1,5},{5,9},{9,... | collective-permute-start | bytes 393224 | tf_op jit(solution)/shard_map/ppermute | solution.py:16
  53.7 1.1 collective-permute-done.4
  54.8 3.0 collective-permute-done.5
  57.8 0.7 subtract_multiply_fusion.5
  58.5 1.3 collective-permute-start.6
  59.8 5.0 %collective-permute-start.7 = (f32[32,1,1024]{2,0,1:T(8,128)S(1)}, f32[32,1,1024]{2,0,1:T(8,128)S(1)}, u32[]{:S(2)}, u32[]{:S(2)}) collective-permute-start(f32[32,1,1024]{2,0,1:T(8,128)S(1)} %get-tuple-element.34), channel_id=1, source_target_pairs={{0,4},{4,8},{8,12},{12,16},{16,20},{20,24},{24,28},{1,5},{5,9},{9,... | collective-permute-start | bytes 393224 | tf_op jit(solution)/shard_map/ppermute | solution.py:16
  65.2 1.3 collective-permute-done.6
  66.5 3.0 collective-permute-done.7
  69.5 0.7 subtract_multiply_fusion.4
  70.2 1.3 collective-permute-start.8
  71.5 5.0 %collective-permute-start.9 = (f32[32,1,1024]{2,0,1:T(8,128)S(1)}, f32[32,1,1024]{2,0,1:T(8,128)S(1)}, u32[]{:S(2)}, u32[]{:S(2)}) collective-permute-start(f32[32,1,1024]{2,0,1:T(8,128)S(1)} %get-tuple-element.30), channel_id=1, source_target_pairs={{0,4},{4,8},{8,12},{12,16},{16,20},{20,24},{24,28},{1,5},{5,9},{9,... | collective-permute-start | bytes 393224 | tf_op jit(solution)/shard_map/ppermute | solution.py:16
  76.9 1.3 collective-permute-done.8
  78.3 3.0 collective-permute-done.9
  81.2 0.7 subtract_multiply_fusion.3
  81.9 1.3 collective-permute-start.10
  83.2 5.0 %collective-permute-start.11 = (f32[32,1,1024]{2,0,1:T(8,128)S(1)}, f32[32,1,1024]{2,0,1:T(8,128)S(1)}, u32[]{:S(2)}, u32[]{:S(2)}) collective-permute-start(f32[32,1,1024]{2,0,1:T(8,128)S(1)} %get-tuple-element.26), channel_id=1, source_target_pairs={{0,4},{4,8},{8,12},{12,16},{16,20},{20,24},{24,28},{1,5},{5,9},{9,... | collective-permute-start | bytes 393224 | tf_op jit(solution)/shard_map/ppermute | solution.py:16
  88.6 1.3 collective-permute-done.10
  90.0 3.0 collective-permute-done.11
  92.9 0.7 subtract_multiply_fusion.2
  93.6 1.3 collective-permute-start.12
  94.9 5.0 %collective-permute-start.13 = (f32[32,1,1024]{2,0,1:T(8,128)S(1)}, f32[32,1,1024]{2,0,1:T(8,128)S(1)}, u32[]{:S(2)}, u32[]{:S(2)}) collective-permute-start(f32[32,1,1024]{2,0,1:T(8,128)S(1)} %get-tuple-element.22), channel_id=1, source_target_pairs={{0,4},{4,8},{8,12},{12,16},{16,20},{20,24},{24,28},{1,5},{5,9},{9,... | collective-permute-start | bytes 393224 | tf_op jit(solution)/shard_map/ppermute | solution.py:16
  100.4 1.3 collective-permute-done.12
  101.7 3.0 collective-permute-done.13
  104.7 0.7 subtract_multiply_fusion.1
  105.4 1.3 collective-permute-start.14
  106.7 5.0 %collective-permute-start.15 = (f32[32,1,1024]{2,0,1:T(8,128)S(1)}, f32[32,1,1024]{2,0,1:T(8,128)S(1)}, u32[]{:S(2)}, u32[]{:S(2)}) collective-permute-start(f32[32,1,1024]{2,0,1:T(8,128)S(1)} %get-tuple-element.18), channel_id=1, source_target_pairs={{0,4},{4,8},{8,12},{12,16},{16,20},{20,24},{24,28},{1,5},{5,9},{9,... | collective-permute-start | bytes 393224 | tf_op jit(solution)/shard_map/ppermute | solution.py:16
  112.1 1.3 collective-permute-done.14
  113.4 3.0 collective-permute-done.15
  116.4 0.7 subtract_multiply_fusion
  117.0 2.7 copy.27
  119.8 2.8 gather_fusion
  122.8 0.7 reshape.71
  123.5 3.2 %all-to-all-start = ((f32[4,1,1024]{2,1,0:T(1,128)}), f32[4,1,1024]{2,1,0:T(1,128)S(1)}, u32[]{:S(2)}, u32[]{:S(2)}) async-start(f32[4,1,1024]{2,1,0:T(1,128)} %reshape.71), calls=%async_computation | async-start | bytes 32768 | tf_op jit(solution)/shard_map/all_to_all | solution.py:92
  126.7 1.0 pad_maximum_fusion.16
  127.8 2.8 all-to-all-done
  130.5 3.5 %all-to-all-start.1 = ((f32[4,32,8,256]{3,1,2,0:T(8,128)}), f32[4,32,8,256]{3,1,2,0:T(8,128)S(1)}, u32[]{:S(2)}, u32[]{:S(2)}) async-start(f32[4,32,8,256]{3,1,2,0:T(8,128)} %pad_maximum_fusion.16), calls=%async_computation.1 | async-start | bytes 2097152 | tf_op jit(solution)/shard_map/all_to_all | solution.py:117
  134.8 0.6 reduce.2
  136.0 0.9 fusion.49
  137.2 44.7 %psum.15 = f32[128]{0:T(128)S(1)} all-reduce(f32[128]{0:T(128)S(1)} %convolution_bitcast_fusion.2), channel_id=1, replica_groups=mesh['slab'=8,'mem'=4] {'slab','mem'}, use_global_device_ids=true, to_apply=%region_3.4 | all-reduce | flops 128 | bytes 1024 | tf_op jit(solution)/shard_map/psum | solution.py:97
  181.9 76.2 %all-reduce.18.cloned.1.call-done = f32[128,128]{1,0:T(8,128)} async-done(((f32[128,128]{1,0:T(8,128)}), f32[128,128]{1,0:T(8,128)}) %all-reduce.18.cloned.1.call-update) | async-done | bytes 65552 | tf_op jit(solution)/shard_map/psum | solution.py:97
  258.0 1.5 select_reduce_fusion
  259.6 1.7 fusion.7
  261.4 1.7 fusion.17
  269.5 1.1 fusion.9
  270.6 0.6 copy.32
  271.2 18.2 %all_to_all.39 = f32[128,8,256]{2,1,0:T(8,128)S(1)} all-to-all(f32[128,8,256]{2,1,0:T(8,128)S(1)} %copy.32), channel_id=1, replica_groups=mesh['slab'=8,'mem'=4] {'mem'}, dimensions={0} | all-to-all | bytes 2097152 | tf_op jit(solution)/shard_map/all_to_all | solution.py:124
  289.4 1.1 copy.33
  (78 shorter events, 11.1 us)
Async XLA Ops:
  6.5 9.8 %copy-start.5 = (s32[128]{0:T(128)S(1)}, s32[128]{0:T(128)}, u32[]{:S(2)}) copy-start(s32[128]{0:T(128)} %param.13) | copy-start | bytes 1540
  6.5 10.4 %copy-start.1 = (f32[8]{0:T(128)S(1)}, f32[8]{0:T(128)}, u32[]{:S(2)}) copy-start(f32[8]{0:T(128)} %param.11) | copy-start | bytes 100
  6.5 11.1 %copy-start = (f32[2,8]{1,0:T(2,128)S(1)}, f32[2,8]{1,0:T(2,128)}, u32[]{:S(2)}) copy-start(f32[2,8]{1,0:T(2,128)} %param.12) | copy-start | bytes 196
  6.5 11.8 %copy-start.2 = (s32[8,1024]{1,0:T(8,128)S(1)}, s32[8,1024]{1,0:T(8,128)}, u32[]{:S(2)}) copy-start(s32[8,1024]{1,0:T(8,128)} %param.10) | copy-start | bytes 98308
  6.5 26.8 %copy-start.3 = (f32[128]{0:T(128)S(1)}, f32[128]{0:T(128)}, u32[]{:S(2)}) copy-start(f32[128]{0:T(128)} %param.15) | copy-start | bytes 1540
  9.2 25.8 %collective-permute-start = (f32[32,1,1024]{2,0,1:T(8,128)}, f32[32,1,1024]{2,0,1:T(8,128)S(1)}, u32[]{:S(2)}, u32[]{:S(2)}) collective-permute-start(f32[32,1,1024]{2,0,1:T(8,128)} %get-tuple-element.47), channel_id=1, source_target_pairs={{4,0},{8,4},{12,8},{16,12},{20,16},{24,20},{28,24},{5,1},{9,5},{13... | collective-permute-start | bytes 393224 | tf_op jit(solution)/shard_map/ppermute | solution.py:19
  10.5 24.5 %collective-permute-start.1 = (f32[32,1,1024]{2,0,1:T(8,128)}, f32[32,1,1024]{2,0,1:T(8,128)S(1)}, u32[]{:S(2)}, u32[]{:S(2)}) collective-permute-start(f32[32,1,1024]{2,0,1:T(8,128)} %get-tuple-element.46), channel_id=1, source_target_pairs={{0,4},{4,8},{8,12},{12,16},{16,20},{20,24},{24,28},{1,5},{5,9},{9,... | collective-permute-start | bytes 393224 | tf_op jit(solution)/shard_map/ppermute | solution.py:16
  35.6 7.8 %collective-permute-start.2 = (f32[32,1,1024]{2,0,1:T(8,128)S(1)}, f32[32,1,1024]{2,0,1:T(8,128)S(1)}, u32[]{:S(2)}, u32[]{:S(2)}) collective-permute-start(f32[32,1,1024]{2,0,1:T(8,128)S(1)} %get-tuple-element.43), channel_id=1, source_target_pairs={{4,0},{8,4},{12,8},{16,12},{20,16},{24,20},{28,24},{5,1},{9,5},{13... | collective-permute-start | bytes 393224 | tf_op jit(solution)/shard_map/ppermute | solution.py:19
  36.9 9.4 %collective-permute-start.3 = (f32[32,1,1024]{2,0,1:T(8,128)S(1)}, f32[32,1,1024]{2,0,1:T(8,128)S(1)}, u32[]{:S(2)}, u32[]{:S(2)}) collective-permute-start(f32[32,1,1024]{2,0,1:T(8,128)S(1)} %get-tuple-element.42), channel_id=1, source_target_pairs={{0,4},{4,8},{8,12},{12,16},{16,20},{20,24},{24,28},{1,5},{5,9},{9,... | collective-permute-start | bytes 393224 | tf_op jit(solution)/shard_map/ppermute | solution.py:16
  47.0 7.8 %collective-permute-start.4 = (f32[32,1,1024]{2,0,1:T(8,128)S(1)}, f32[32,1,1024]{2,0,1:T(8,128)S(1)}, u32[]{:S(2)}, u32[]{:S(2)}) collective-permute-start(f32[32,1,1024]{2,0,1:T(8,128)S(1)} %get-tuple-element.39), channel_id=1, source_target_pairs={{4,0},{8,4},{12,8},{16,12},{20,16},{24,20},{28,24},{5,1},{9,5},{13... | collective-permute-start | bytes 393224 | tf_op jit(solution)/shard_map/ppermute | solution.py:19
  48.3 9.5 %collective-permute-start.5 = (f32[32,1,1024]{2,0,1:T(8,128)S(1)}, f32[32,1,1024]{2,0,1:T(8,128)S(1)}, u32[]{:S(2)}, u32[]{:S(2)}) collective-permute-start(f32[32,1,1024]{2,0,1:T(8,128)S(1)} %get-tuple-element.38), channel_id=1, source_target_pairs={{0,4},{4,8},{8,12},{12,16},{16,20},{20,24},{24,28},{1,5},{5,9},{9,... | collective-permute-start | bytes 393224 | tf_op jit(solution)/shard_map/ppermute | solution.py:16
  58.5 8.1 %collective-permute-start.6 = (f32[32,1,1024]{2,0,1:T(8,128)S(1)}, f32[32,1,1024]{2,0,1:T(8,128)S(1)}, u32[]{:S(2)}, u32[]{:S(2)}) collective-permute-start(f32[32,1,1024]{2,0,1:T(8,128)S(1)} %get-tuple-element.35), channel_id=1, source_target_pairs={{4,0},{8,4},{12,8},{16,12},{20,16},{24,20},{28,24},{5,1},{9,5},{13... | collective-permute-start | bytes 393224 | tf_op jit(solution)/shard_map/ppermute | solution.py:19
  59.8 9.7 %collective-permute-start.7 = (f32[32,1,1024]{2,0,1:T(8,128)S(1)}, f32[32,1,1024]{2,0,1:T(8,128)S(1)}, u32[]{:S(2)}, u32[]{:S(2)}) collective-permute-start(f32[32,1,1024]{2,0,1:T(8,128)S(1)} %get-tuple-element.34), channel_id=1, source_target_pairs={{0,4},{4,8},{8,12},{12,16},{16,20},{20,24},{24,28},{1,5},{5,9},{9,... | collective-permute-start | bytes 393224 | tf_op jit(solution)/shard_map/ppermute | solution.py:16
  70.2 8.1 %collective-permute-start.8 = (f32[32,1,1024]{2,0,1:T(8,128)S(1)}, f32[32,1,1024]{2,0,1:T(8,128)S(1)}, u32[]{:S(2)}, u32[]{:S(2)}) collective-permute-start(f32[32,1,1024]{2,0,1:T(8,128)S(1)} %get-tuple-element.31), channel_id=1, source_target_pairs={{4,0},{8,4},{12,8},{16,12},{20,16},{24,20},{28,24},{5,1},{9,5},{13... | collective-permute-start | bytes 393224 | tf_op jit(solution)/shard_map/ppermute | solution.py:19
  71.5 9.7 %collective-permute-start.9 = (f32[32,1,1024]{2,0,1:T(8,128)S(1)}, f32[32,1,1024]{2,0,1:T(8,128)S(1)}, u32[]{:S(2)}, u32[]{:S(2)}) collective-permute-start(f32[32,1,1024]{2,0,1:T(8,128)S(1)} %get-tuple-element.30), channel_id=1, source_target_pairs={{0,4},{4,8},{8,12},{12,16},{16,20},{20,24},{24,28},{1,5},{5,9},{9,... | collective-permute-start | bytes 393224 | tf_op jit(solution)/shard_map/ppermute | solution.py:16
  81.9 8.1 %collective-permute-start.10 = (f32[32,1,1024]{2,0,1:T(8,128)S(1)}, f32[32,1,1024]{2,0,1:T(8,128)S(1)}, u32[]{:S(2)}, u32[]{:S(2)}) collective-permute-start(f32[32,1,1024]{2,0,1:T(8,128)S(1)} %get-tuple-element.27), channel_id=1, source_target_pairs={{4,0},{8,4},{12,8},{16,12},{20,16},{24,20},{28,24},{5,1},{9,5},{13... | collective-permute-start | bytes 393224 | tf_op jit(solution)/shard_map/ppermute | solution.py:19
  83.2 9.7 %collective-permute-start.11 = (f32[32,1,1024]{2,0,1:T(8,128)S(1)}, f32[32,1,1024]{2,0,1:T(8,128)S(1)}, u32[]{:S(2)}, u32[]{:S(2)}) collective-permute-start(f32[32,1,1024]{2,0,1:T(8,128)S(1)} %get-tuple-element.26), channel_id=1, source_target_pairs={{0,4},{4,8},{8,12},{12,16},{16,20},{20,24},{24,28},{1,5},{5,9},{9,... | collective-permute-start | bytes 393224 | tf_op jit(solution)/shard_map/ppermute | solution.py:16
  93.6 8.1 %collective-permute-start.12 = (f32[32,1,1024]{2,0,1:T(8,128)S(1)}, f32[32,1,1024]{2,0,1:T(8,128)S(1)}, u32[]{:S(2)}, u32[]{:S(2)}) collective-permute-start(f32[32,1,1024]{2,0,1:T(8,128)S(1)} %get-tuple-element.23), channel_id=1, source_target_pairs={{4,0},{8,4},{12,8},{16,12},{20,16},{24,20},{28,24},{5,1},{9,5},{13... | collective-permute-start | bytes 393224 | tf_op jit(solution)/shard_map/ppermute | solution.py:19
  94.9 9.7 %collective-permute-start.13 = (f32[32,1,1024]{2,0,1:T(8,128)S(1)}, f32[32,1,1024]{2,0,1:T(8,128)S(1)}, u32[]{:S(2)}, u32[]{:S(2)}) collective-permute-start(f32[32,1,1024]{2,0,1:T(8,128)S(1)} %get-tuple-element.22), channel_id=1, source_target_pairs={{0,4},{4,8},{8,12},{12,16},{16,20},{20,24},{24,28},{1,5},{5,9},{9,... | collective-permute-start | bytes 393224 | tf_op jit(solution)/shard_map/ppermute | solution.py:16
  105.4 8.1 %collective-permute-start.14 = (f32[32,1,1024]{2,0,1:T(8,128)S(1)}, f32[32,1,1024]{2,0,1:T(8,128)S(1)}, u32[]{:S(2)}, u32[]{:S(2)}) collective-permute-start(f32[32,1,1024]{2,0,1:T(8,128)S(1)} %get-tuple-element.19), channel_id=1, source_target_pairs={{4,0},{8,4},{12,8},{16,12},{20,16},{24,20},{28,24},{5,1},{9,5},{13... | collective-permute-start | bytes 393224 | tf_op jit(solution)/shard_map/ppermute | solution.py:19
  106.7 9.7 %collective-permute-start.15 = (f32[32,1,1024]{2,0,1:T(8,128)S(1)}, f32[32,1,1024]{2,0,1:T(8,128)S(1)}, u32[]{:S(2)}, u32[]{:S(2)}) collective-permute-start(f32[32,1,1024]{2,0,1:T(8,128)S(1)} %get-tuple-element.18), channel_id=1, source_target_pairs={{0,4},{4,8},{8,12},{12,16},{16,20},{20,24},{24,28},{1,5},{5,9},{9,... | collective-permute-start | bytes 393224 | tf_op jit(solution)/shard_map/ppermute | solution.py:16
  119.7 17.3 %copy-start.4 = (f32[128]{0:T(128)S(1)}, f32[128]{0:T(128)}, u32[]{:S(2)}) copy-start(f32[128]{0:T(128)} %param.15) | copy-start | bytes 1540
  119.7 17.3 %copy-start.6 = (f32[128]{0:T(128)S(1)}, f32[128]{0:T(128)}, u32[]{:S(2)}) copy-start(f32[128]{0:T(128)} %param.14) | copy-start | bytes 1540
  123.5 7.1 %all-to-all-start = ((f32[4,1,1024]{2,1,0:T(1,128)}), f32[4,1,1024]{2,1,0:T(1,128)S(1)}, u32[]{:S(2)}, u32[]{:S(2)}) async-start(f32[4,1,1024]{2,1,0:T(1,128)} %reshape.71), calls=%async_computation | async-start | bytes 32768 | tf_op jit(solution)/shard_map/all_to_all | solution.py:92
  130.5 138.8 %all-to-all-start.1 = ((f32[4,32,8,256]{3,1,2,0:T(8,128)}), f32[4,32,8,256]{3,1,2,0:T(8,128)S(1)}, u32[]{:S(2)}, u32[]{:S(2)}) async-start(f32[4,32,8,256]{3,1,2,0:T(8,128)} %pad_maximum_fusion.16), calls=%async_computation.1 | async-start | bytes 2097152 | tf_op jit(solution)/shard_map/all_to_all | solution.py:117
  134.1 124.0 %all-reduce.18.cloned.1.call-start = ((), (), s32[]{:S(2)}) async-start(), calls=%async_computation.3 | async-start | bytes 131072 | tf_op jit(solution)/shard_map/psum | solution.py:97
Sparse Core Ops, SparseCore 0:
  140.5 117.4 all-reduce.17
